TPU v7x, 32 devices: a whole 2x2x4 slice. The times are simulated.
32 devices in a mesh: rows: 4 (over y, x), cols: 8 (over z, core).
Axes of the slice: x: 2, y: 2, z: 4, core: 2. Of those that a mesh axis runs over, the one named last changes fastest.
Arguments:
- data_tile: bfloat16 [1024, 8192], P('rows', 'cols'), may hold values from 0.05 to 5
- w_factor: float32 [32, 1024], P(None, ('rows', 'cols')), may hold values from 0.05 to 0.5
- h_factor: float32 [32, 8192], P(None, ('cols', 'rows')), may hold values from 0.05 to 0.5
Outputs:
- w_final: float32 [32, 1024], P(None, ('rows', 'cols'))
- h_final: float32 [32, 8192], P(None, ('cols', 'rows'))
All inputs are finite; a program needn't handle non-finite values.
Results may differ from a plain program's by a relative error of at most 0.00049.
Values may be sent and summed in bfloat16 or wider, within the bound.
A program may use at most 64 MiB of HBM per device.

v0:
```python
import jax
import jax.numpy as jnp
from jax import lax
from jax.sharding import PartitionSpec as P

ITERS = 2
damping = 0.75


def quotient_terms(data_tile, w_block, h_block):
    approx = jnp.einsum("ki,kj->ij", w_block, h_block, preferred_element_type=jnp.float32)
    quotient = (data_tile.astype(jnp.float32) / approx).astype(jnp.bfloat16)
    h_part = jnp.einsum("ki,ij->kj", w_block, quotient, preferred_element_type=jnp.float32)
    w_part = jnp.einsum("kj,ij->ki", h_block, quotient, preferred_element_type=jnp.float32)
    return (h_part, w_part)


def row_sums(block):
    return jnp.sum(block.astype(jnp.float32), axis=1)


def totals(w_own, h_own):
    w_total, h_total = lax.psum((row_sums(w_own), row_sums(h_own)), ("rows", "cols"))
    return (w_total, h_total)


def scaled(factor, numer, total):
    return factor * (1.0 - damping + damping * numer / total[:, None])


def shards(data_tile, w_factor, h_factor):
    w_now = w_factor
    h_now = h_factor
    for rounds in range(ITERS):
        w_round = w_now.astype(jnp.bfloat16)
        h_round = h_now.astype(jnp.bfloat16)
        w_block = lax.all_gather(w_round, "cols", axis=1, tiled=True)
        h_block = lax.all_gather(h_round, "rows", axis=1, tiled=True)
        h_part, w_part = quotient_terms(data_tile, w_block, h_block)
        h_numer = lax.psum_scatter(h_part, "rows", scatter_dimension=1, tiled=True)
        w_numer = lax.psum_scatter(w_part, "cols", scatter_dimension=1, tiled=True)
        w_total, h_total = totals(w_round, h_round)
        h_next = scaled(h_now, h_numer, w_total)
        w_next = scaled(w_now, w_numer, h_total)
        w_now = w_next
        h_now = h_next
    return (w_now, h_now)


def solution(mesh):
    placed = (P("rows", "cols"), P(None, ("rows", "cols")), P(None, ("cols", "rows")))
    return jax.shard_map(
        shards,
        mesh=mesh,
        in_specs=placed,
        out_specs=(P(None, ("rows", "cols")), P(None, ("cols", "rows"))),
        check_vma=False,
    )
```

profile of v0, /device:TPU:0, one launch (start us, length us, event | category | flops | bytes accessed | tf_op | source)
XLA Modules:
  0.0 165.2 jit_solution(12160451287689017585)
XLA Ops:
  7.2 0.0 reduce-scatter.13.cloned.1.call-start
  7.2 0.9 convert_reduce_fusion.1
  8.1 0.0 copy-start.1
  8.1 10.1 %all_gather.13 = bf16[32,1024]{1,0:T(8,128)(2,1)S(1)} all-gather(bf16[32,256]{1,0:T(8,128)(2,1)S(1)} %get-tuple-element.11), channel_id=1, replica_groups=mesh['rows'=4,'cols'=8] {'rows'}, dimensions={1}, use_global_device_ids=true | all-gather | bytes 81920 | tf_op jit(solution)/shard_map/all_gather | solution.py:38
  18.2 0.0 copy-done.1
  18.2 0.1 copy.5
  18.2 14.2 %all_gather.12 = bf16[32,256]{0,1:T(8,128)(2,1)S(1)} all-gather(bf16[32,32]{0,1:T(8,128)(2,1)S(1)} %copy.5), channel_id=1, replica_groups=mesh['rows'=4,'cols'=8] {'cols'}, dimensions={1}, use_global_device_ids=true | all-gather | bytes 18432 | tf_op jit(solution)/shard_map/all_gather | solution.py:37
  32.4 1.3 fusion
  33.8 0.2 convolution_bitcast_fusion.2
  34.0 0.8 copy.7
  34.8 0.0 reduce-scatter.13.cloned.1.call-update
  34.8 0.0 copy-start.3
  34.8 0.0 reduce-scatter.9.cloned.1.call-start
  34.9 0.9 convolution_bitcast_fusion.1
  35.8 0.0 reduce-scatter.9.cloned.1.call-update
  35.8 0.0 reduce-scatter.15.cloned.1.call-start
  35.9 39.3 %all-reduce.1 = (f32[32]{0:T(128)S(1)}, f32[32]{0:T(128)S(1)}) all-reduce(f32[32]{0:T(128)S(1)} %convert_reduce_fusion.3, f32[32]{0:T(128)S(1)} %get-tuple-element.10), channel_id=1, replica_groups=mesh['rows'=4,'cols'=8] {'rows','cols'}, use_global_device_ids=true, to_apply=%region_5.0 | all-reduce | flops 64 | bytes 512 | tf_op jit(solution)/shard_map/psum | solution.py:23
  75.2 0.0 reduce-scatter.13.cloned.1.call-done
  75.2 0.8 copy.8
  76.0 0.2 convert_reduce_fusion.2
  76.2 0.1 copy.6
  76.2 0.0 copy-start
  76.2 14.1 %all_gather.15 = bf16[32,256]{0,1:T(8,128)(2,1)S(1)} all-gather(bf16[32,32]{0,1:T(8,128)(2,1)S(1)} %copy.6), channel_id=1, replica_groups=mesh['rows'=4,'cols'=8] {'cols'}, dimensions={1}, use_global_device_ids=true | all-gather | bytes 18432 | tf_op jit(solution)/shard_map/all_gather | solution.py:37
  90.4 0.4 reduce-scatter.9.cloned.1.call-done
  90.8 0.0 copy-done
  90.8 0.9 convert_reduce_fusion
  91.7 8.8 %all_gather.14 = bf16[32,1024]{1,0:T(8,128)(2,1)S(1)} all-gather(bf16[32,256]{1,0:T(8,128)(2,1)S(1)} %get-tuple-element.9), channel_id=1, replica_groups=mesh['rows'=4,'cols'=8] {'rows'}, dimensions={1}, use_global_device_ids=true | all-gather | bytes 81920 | tf_op jit(solution)/shard_map/all_gather | solution.py:38
  100.5 0.0 copy-done.3
  100.5 0.3 fusion.1
  100.8 0.9 convolution_bitcast_fusion
  101.7 0.0 reduce-scatter.15.cloned.1.call-update
  101.7 0.0 reduce-scatter.11.cloned.1.call-start
  101.8 0.9 fusion.6
  102.7 0.0 reduce-scatter.11.cloned.1.call-update
  102.7 39.0 %all-reduce = (f32[32]{0:T(128)S(1)}, f32[32]{0:T(128)S(1)}) all-reduce(f32[32]{0:T(128)S(1)} %get-tuple-element.8, f32[32]{0:T(128)S(1)} %get-tuple-element.6), channel_id=1, replica_groups=mesh['rows'=4,'cols'=8] {'rows','cols'}, use_global_device_ids=true, to_apply=%region_8.0 | all-reduce | flops 64 | bytes 512 | tf_op jit(solution)/shard_map/psum | solution.py:23
  141.7 0.0 reduce-scatter.15.cloned.1.call-done
  141.7 0.8 copy.10
  142.5 0.0 copy-start.2
  142.5 0.7 add_multiply_fusion.2
  143.2 14.1 %reduce-scatter.11.cloned.1.call-done = f32[32,256]{1,0:T(8,128)} async-done(((f32[32,1024]{1,0:T(8,128)}), f32[32,256]{1,0:T(8,128)}) %reduce-scatter.11.cloned.1.call-update) | async-done | bytes 32784 | tf_op jit(solution)/shard_map/reduce_scatter | solution.py:40
  157.2 0.0 copy-done.2
  157.2 1.5 add_multiply_fusion
  (1 shorter events, 0.0 us)
Async XLA Ops:
  7.2 68.0 %reduce-scatter.13.cloned.1.call-start = ((), (), s32[]{:S(2)}) async-start(), calls=%async_computation.6 | async-start | bytes 147456
  8.1 10.1 %copy-start.1 = (f32[32,32]{1,0:T(8,128)S(1)}, f32[32,32]{1,0:T(8,128)}, u32[]{:S(2)}) copy-start(f32[32,32]{1,0:T(8,128)} %param.4) | copy-start | bytes 12292
  34.8 65.7 %copy-start.3 = (bf16[256,1024]{1,0:T(8,128)(2,1)S(1)}, bf16[256,1024]{1,0:T(8,128)(2,1)}, u32[]{:S(2)}) copy-start(bf16[256,1024]{1,0:T(8,128)(2,1)} %param.3) | copy-start | bytes 1572868
  34.8 55.9 %reduce-scatter.9.cloned.1.call-start = ((), (), s32[]{:S(2)}) async-start(), calls=%async_computation.4 | async-start | bytes 163840 | tf_op jit(solution)/shard_map/reduce_scatter | solution.py:40
  35.8 105.9 %reduce-scatter.15.cloned.1.call-start = ((), (), s32[]{:S(2)}) async-start(), calls=%async_computation.7 | async-start | bytes 147456
  76.2 14.5 %copy-start = (f32[32,256]{1,0:T(8,128)S(1)}, f32[32,256]{1,0:T(8,128)}, u32[]{:S(2)}) copy-start(f32[32,256]{1,0:T(8,128)} %param.5) | copy-start | bytes 98308
  101.7 55.5 %reduce-scatter.11.cloned.1.call-start = ((), (), s32[]{:S(2)}) async-start(), calls=%async_computation.5 | async-start | bytes 163840 | tf_op jit(solution)/shard_map/reduce_scatter | solution.py:40
  142.5 14.8 %copy-start.2 = (f32[32,256]{1,0:T(8,128)S(1)}, f32[32,256]{1,0:T(8,128)}, u32[]{:S(2)}) copy-start(f32[32,256]{1,0:T(8,128)} %reduce-scatter.9.cloned.1.call-done) | copy-start | bytes 98308
Sparse Core Ops, SparseCore 0:
  34.9 30.7 reduce-scatter.12
  68.4 22.2 reduce-scatter.8
  101.9 30.2 reduce-scatter.14
  134.7 22.4 reduce-scatter.10
where the time goes:
time: 166 us; the launch traced here: 165 us
  blocking collectives  126 us (76%)
  waiting for transfers between devices  14.5 us (9%)
  between operations  13.8 us (8%)
  matrix products  4.5 us (3%)
  other arithmetic  4.17 us (3%)
  local copies, waits for them, and re-layouts  2.53 us (2%)
    psum x2, blocking collectives, totals(): lax.psum((row_sums(w_own), row_sums(h_own)), ('rows', 'cols'))  78.3 us
    all_gather x2, blocking collectives, shards(): w_block = lax.all_gather(w_round, 'cols', axis=1, tiled=True)  28.3 us
    all_gather x2, blocking collectives, shards(): h_block = lax.all_gather(h_round, 'rows', axis=1, tiled=True)  18.9 us
    reduce_scatter x2, waiting for transfers between devices, shards(): h_numer = lax.psum_scatter(h_part, 'rows', scatter_dimension=1, tiled=True)  14.5 us
  transfers between devices with their start and end apart: 4, of which 2 were waited for; matrix products, arithmetic and copies ran while one was open for 3% of the time, Pallas kernels for 0%

commit v1 on v0

--- a/solution.py
+++ b/solution.py
@@ -34,7 +34,8 @@
     for rounds in range(ITERS):
         w_round = w_now.astype(jnp.bfloat16)
         h_round = h_now.astype(jnp.bfloat16)
-        w_block = lax.all_gather(w_round, "cols", axis=1, tiled=True)
+        parts = lax.all_gather(w_round, "cols", axis=0, tiled=False)
+        w_block = jnp.concatenate(parts, axis=1)
         h_block = lax.all_gather(h_round, "rows", axis=1, tiled=True)
         h_part, w_part = quotient_terms(data_tile, w_block, h_block)
         h_numer = lax.psum_scatter(h_part, "rows", scatter_dimension=1, tiled=True)

time: 166 us -> 167 us (level)
  no operation moved by 1% of the time
where the time goes in v1:
time: 167 us; the launch traced here: 166 us
  blocking collectives  125 us (75%)
  waiting for transfers between devices  14.5 us (9%)
  between operations  13.8 us (8%)
  other arithmetic  4.98 us (3%)
  matrix products  4.57 us (3%)
  local copies, waits for them, and re-layouts  2.77 us (2%)
    psum x2, blocking collectives, totals(): lax.psum((row_sums(w_own), row_sums(h_own)), ('rows', 'cols'))  77.7 us
    all_gather x2, blocking collectives, shards(): parts = lax.all_gather(w_round, 'cols', axis=0, tiled=False)  29.7 us
    all_gather x2, blocking collectives, shards(): h_block = lax.all_gather(h_round, 'rows', axis=1, tiled=True)  17.7 us
    reduce_scatter x2, waiting for transfers between devices, shards(): h_numer = lax.psum_scatter(h_part, 'rows', scatter_dimension=1, tiled=True)  14.4 us
  transfers between devices with their start and end apart: 4, of which 2 were waited for; matrix products, arithmetic and copies ran while one was open for 3% of the time, Pallas kernels for 0%

profile of v1, /device:TPU:0, one launch (start us, length us, event | category | flops | bytes accessed | tf_op | source)
XLA Modules:
  0.0 165.9 jit_solution(5111842173575938902)
XLA Ops:
  7.2 0.0 reduce-scatter.13.cloned.1.call-start
  7.2 0.8 convert_reduce_fusion.3
  8.0 0.9 convert_reduce_fusion.1
  8.9 15.7 %all-gather = bf16[256,32]{1,0:T(8,128)(2,1)S(1)} all-gather(bf16[32,32]{1,0:T(8,128)(2,1)S(1)} %get-tuple-element.13), channel_id=2, replica_groups=mesh['rows'=4,'cols'=8] {'cols'}, dimensions={0}, use_global_device_ids=true | all-gather | bytes 18432 | tf_op jit(solution)/shard_map/all_gather | solution.py:37
  24.6 0.1 reshape.21
  24.7 8.5 %all_gather.20 = bf16[32,1024]{1,0:T(8,128)(2,1)S(1)} all-gather(bf16[32,256]{1,0:T(8,128)(2,1)S(1)} %get-tuple-element.11), channel_id=1, replica_groups=mesh['rows'=4,'cols'=8] {'rows'}, dimensions={1}, use_global_device_ids=true | all-gather | bytes 81920 | tf_op jit(solution)/shard_map/all_gather | solution.py:39
  33.2 1.4 fusion
  34.6 0.3 convolution_bitcast_fusion.2
  34.8 0.8 copy.9
  35.6 0.0 reduce-scatter.13.cloned.1.call-update
  35.6 0.0 copy-start.3
  35.6 0.0 reduce-scatter.9.cloned.1.call-start
  35.7 0.8 convolution_bitcast_fusion
  36.5 0.0 reduce-scatter.9.cloned.1.call-update
  36.5 0.0 reduce-scatter.15.cloned.1.call-start
  36.6 39.3 %all-reduce.1 = (f32[32]{0:T(128)S(1)}, f32[32]{0:T(128)S(1)}) all-reduce(f32[32]{0:T(128)S(1)} %get-tuple-element.12, f32[32]{0:T(128)S(1)} %get-tuple-element.10), channel_id=1, replica_groups=mesh['rows'=4,'cols'=8] {'rows','cols'}, use_global_device_ids=true, to_apply=%region_5.0 | all-reduce | flops 64 | bytes 512 | tf_op jit(solution)/shard_map/psum | solution.py:23
  75.9 0.0 reduce-scatter.13.cloned.1.call-done
  75.9 0.0 copy-start.1
  75.9 0.8 copy.10
  76.7 0.0 copy-done.1
  76.7 0.2 convert_reduce_fusion.2
  76.9 14.0 %all-gather.1 = bf16[256,32]{1,0:T(8,128)(2,1)S(1)} all-gather(bf16[32,32]{1,0:T(8,128)(2,1)S(1)} %get-tuple-element.7), channel_id=3, replica_groups=mesh['rows'=4,'cols'=8] {'cols'}, dimensions={0}, use_global_device_ids=true | all-gather | bytes 18432 | tf_op jit(solution)/shard_map/all_gather | solution.py:37
  90.9 0.0 copy-start
  91.0 0.1 reshape.23
  91.1 0.5 reduce-scatter.9.cloned.1.call-done
  91.6 0.1 copy-done
  91.7 0.9 convert_reduce_fusion
  92.7 9.2 %all_gather.21 = bf16[32,1024]{1,0:T(8,128)(2,1)S(1)} all-gather(bf16[32,256]{1,0:T(8,128)(2,1)S(1)} %get-tuple-element.9), channel_id=1, replica_groups=mesh['rows'=4,'cols'=8] {'rows'}, dimensions={1}, use_global_device_ids=true | all-gather | bytes 81920 | tf_op jit(solution)/shard_map/all_gather | solution.py:39
  101.9 0.0 copy-done.3
  101.9 0.3 fusion.1
  102.2 0.9 convolution_bitcast_fusion.1
  103.1 0.0 reduce-scatter.15.cloned.1.call-update
  103.1 0.0 reduce-scatter.11.cloned.1.call-start
  103.2 0.9 fusion.6
  104.0 0.0 reduce-scatter.11.cloned.1.call-update
  104.1 38.4 %all-reduce = (f32[32]{0:T(128)S(1)}, f32[32]{0:T(128)S(1)}) all-reduce(f32[32]{0:T(128)S(1)} %get-tuple-element.8, f32[32]{0:T(128)S(1)} %get-tuple-element.6), channel_id=1, replica_groups=mesh['rows'=4,'cols'=8] {'rows','cols'}, use_global_device_ids=true, to_apply=%region_8.0 | all-reduce | flops 64 | bytes 512 | tf_op jit(solution)/shard_map/psum | solution.py:23
  142.5 0.0 reduce-scatter.15.cloned.1.call-done
  142.5 0.8 copy.12
  143.3 0.0 copy-start.2
  143.3 0.7 add_multiply_fusion.2
  144.0 13.9 %reduce-scatter.11.cloned.1.call-done = f32[32,256]{1,0:T(8,128)} async-done(((f32[32,1024]{1,0:T(8,128)}), f32[32,256]{1,0:T(8,128)}) %reduce-scatter.11.cloned.1.call-update) | async-done | bytes 32784 | tf_op jit(solution)/shard_map/reduce_scatter | solution.py:41
  157.9 0.0 copy-done.2
  157.9 1.5 add_multiply_fusion
  (2 shorter events, 0.1 us)
Async XLA Ops:
  7.2 68.8 %reduce-scatter.13.cloned.1.call-start = ((), (), s32[]{:S(2)}) async-start(), calls=%async_computation.6 | async-start | bytes 147456
  35.6 66.2 %copy-start.3 = (bf16[256,1024]{1,0:T(8,128)(2,1)S(1)}, bf16[256,1024]{1,0:T(8,128)(2,1)}, u32[]{:S(2)}) copy-start(bf16[256,1024]{1,0:T(8,128)(2,1)} %param.3) | copy-start | bytes 1572868
  35.6 55.9 %reduce-scatter.9.cloned.1.call-start = ((), (), s32[]{:S(2)}) async-start(), calls=%async_computation.4 | async-start | bytes 163840 | tf_op jit(solution)/shard_map/reduce_scatter | solution.py:41
  36.5 105.9 %reduce-scatter.15.cloned.1.call-start = ((), (), s32[]{:S(2)}) async-start(), calls=%async_computation.7 | async-start | bytes 147456
  75.9 0.8 copy-start.1
  90.9 0.8 copy-start
  103.1 54.7 %reduce-scatter.11.cloned.1.call-start = ((), (), s32[]{:S(2)}) async-start(), calls=%async_computation.5 | async-start | bytes 163840 | tf_op jit(solution)/shard_map/reduce_scatter | solution.py:41
  143.3 14.6 %copy-start.2 = (f32[32,256]{1,0:T(8,128)S(1)}, f32[32,256]{1,0:T(8,128)}, u32[]{:S(2)}) copy-start(f32[32,256]{1,0:T(8,128)} %reduce-scatter.9.cloned.1.call-done) | copy-start | bytes 98308
Sparse Core Ops, SparseCore 0:
  35.7 30.6 reduce-scatter.12
  69.2 22.3 reduce-scatter.8
  103.3 29.6 reduce-scatter.14
  135.6 22.2 reduce-scatter.10
